TPU v7x, 512 devices: a whole 4x8x8 slice. The times are simulated.
512 devices in a mesh: interval: 8 (over y), seq: 8 (over x, core), head: 8 (over z).
Axes of the slice: x: 4, y: 8, z: 8, core: 2. Of those that a mesh axis runs over, the one named last changes fastest.
Arguments:
- hidden_in: bfloat16 [8, 2048, 1536], P('interval', 'seq'), may hold values from -6 to 6
- ctx_grad: bfloat16 [8, 2048, 1536], P('interval', 'seq', 'head'), may hold values from -6 to 6
- w_query: bfloat16 [1536, 1536], P('head'), may hold values from -0.15625 to 0.15625
- w_key: bfloat16 [1536, 1536], P('head'), may hold values from -0.15625 to 0.15625
- w_value: bfloat16 [1536, 1536], P('head'), may hold values from -0.15625 to 0.15625
- w_junction: bfloat16 [1536, 128], replicated, may hold values from -0.15625 to 0.15625
- donor_pos: int32 [8, 8, 8, 64], P('interval', 'seq', None, 'head'), may hold values from 0 to 255
- acceptor_pos: int32 [8, 8, 8, 64], P('interval', 'seq', None, 'head'), may hold values from 0 to 255
- junction_counts: int32 [8, 8, 8], P('interval', 'seq'), may hold values from 16 to 64, as said below
- pred_grad: float32 [8, 8, 8, 64], P('interval', 'seq', None, 'head'), may hold values from -6 to 6
Outputs:
- grad_input: bfloat16 [8, 2048, 1536], P('interval', 'seq', 'head')
- grad_query: bfloat16 [1536, 1536], P('head')
- grad_key: bfloat16 [1536, 1536], P('head')
- grad_value: bfloat16 [1536, 1536], P('head')
Inputs may be any that keep to these rules, and one draw needn't show every extreme that they name: `junction_counts`: slots at or past a bucket's count are empty. In each interval one acceptor shard, drawn from the seed, has 64 live slots from every donor shard; every other bucket has 16 to 32.
All inputs are finite; a program needn't handle non-finite values.
Results may differ from a plain program's by a relative error of at most 0.022.
Values may be sent and summed in bfloat16 or wider, within the bound.
No kernel may reach another device: no remote copies, remote signals or barrier semaphores. Data moves between devices by JAX's collectives and lax.ppermute only.
A program may use at most 64 MiB of HBM per device.

v0:
```python
import jax
import jax.numpy as jnp
from jax import lax
from jax.sharding import PartitionSpec as P

HD = 192
PJ = 128


def on_device(
    hidden_in,
    ctx_grad,
    w_query,
    w_key,
    w_value,
    w_junction,
    donor_pos,
    acceptor_pos,
    junction_counts,
    pred_grad,
):
    hidden = hidden_in[0]
    local_len = hidden.shape[0]
    shard_count = lax.axis_size("seq")
    total_len = local_len * shard_count
    heads_dev = w_query.shape[0] // HD
    softmax_scale = HD ** (-0.5)
    pair_scale = PJ ** (-0.5)
    queries = jnp.einsum("td,cd->tc", hidden, w_query, preferred_element_type=jnp.float32).astype(
        jnp.bfloat16
    )
    key_rows = jnp.einsum("td,cd->tc", hidden, w_key, preferred_element_type=jnp.float32).astype(
        jnp.bfloat16
    )
    value_rows = jnp.einsum(
        "td,cd->tc", hidden, w_value, preferred_element_type=jnp.float32
    ).astype(jnp.bfloat16)
    features = jnp.dot(hidden, w_junction, preferred_element_type=jnp.float32).astype(jnp.bfloat16)
    all_keys, all_values, all_features = (
        lax.all_gather(key_rows, "seq", axis=0, tiled=True),
        lax.all_gather(value_rows, "seq", axis=0, tiled=True),
        lax.all_gather(features, "seq", axis=0, tiled=True),
    )
    query_heads = queries.reshape(local_len, heads_dev, HD)
    grad_heads = ctx_grad[0].reshape(local_len, heads_dev, HD)
    key_heads = all_keys.reshape(total_len, heads_dev, HD)
    value_heads = all_values.reshape(total_len, heads_dev, HD)
    scores = (
        jnp.einsum("qhd,khd->hqk", query_heads, key_heads, preferred_element_type=jnp.float32)
        * softmax_scale
    )
    row_max = jnp.max(scores, axis=-1, keepdims=True)
    expd = jnp.exp(scores - row_max)
    probs = expd / jnp.sum(expd, axis=-1, keepdims=True)
    dprobs = jnp.einsum("qhd,khd->hqk", grad_heads, value_heads, preferred_element_type=jnp.float32)
    row_delta = jnp.sum(probs * dprobs, axis=-1, keepdims=True)
    dscores = probs * (dprobs - row_delta)
    probs_b = probs.astype(jnp.bfloat16)
    dscores_b = dscores.astype(jnp.bfloat16)
    query_grad = (
        (
            jnp.einsum("hqk,khd->qhd", dscores_b, key_heads, preferred_element_type=jnp.float32)
            * softmax_scale
        )
        .astype(jnp.bfloat16)
        .reshape(local_len, heads_dev * HD)
    )
    key_term = (
        jnp.einsum("hqk,qhd->khd", dscores_b, query_heads, preferred_element_type=jnp.float32)
        * softmax_scale
    ).reshape(total_len, heads_dev * HD)
    value_term = jnp.einsum(
        "hqk,qhd->khd", probs_b, grad_heads, preferred_element_type=jnp.float32
    ).reshape(total_len, heads_dev * HD)
    key_sum, value_sum = (
        lax.psum_scatter(
            key_term.astype(jnp.bfloat16), "seq", scatter_dimension=0, tiled=True
        ).astype(jnp.float32),
        lax.psum_scatter(
            value_term.astype(jnp.bfloat16), "seq", scatter_dimension=0, tiled=True
        ).astype(jnp.float32),
    )
    key_grad = key_sum.astype(jnp.bfloat16)
    value_grad = value_sum.astype(jnp.bfloat16)
    donor_idx = donor_pos[0, 0]
    accept_idx = acceptor_pos[0, 0]
    slot_dev = donor_idx.shape[1]
    slot_ids = lax.axis_index("head") * slot_dev + jnp.arange(slot_dev, dtype=jnp.int32)
    live_slots = slot_ids[None, :] < junction_counts[0, 0][:, None]
    donor_feat = features[donor_idx].astype(jnp.float32)
    accept_glob = jnp.arange(shard_count, dtype=jnp.int32)[:, None] * local_len + accept_idx
    accept_rows = all_features[accept_glob]
    accept_feat = accept_rows.astype(jnp.float32)
    pair_score = jnp.sum(donor_feat * accept_feat, axis=-1) * pair_scale
    slot_grad = (
        jnp.where(live_slots, pred_grad[0, 0] * jax.nn.sigmoid(pair_score), 0.0) * pair_scale
    )
    donor_term = slot_grad[..., None] * accept_feat
    accept_term = slot_grad[..., None] * donor_feat
    pair_width = features.shape[1]
    grad_feat = (
        jnp.zeros((local_len, pair_width), jnp.float32)
        .at[donor_idx.reshape(-1)]
        .add(donor_term.reshape(-1, pair_width))
    )
    spread_term = (
        jnp.zeros((total_len, pair_width), jnp.float32)
        .at[accept_glob.reshape(-1)]
        .add(accept_term.reshape(-1, pair_width))
    )
    grad_feat = grad_feat + lax.psum_scatter(
        spread_term.astype(jnp.bfloat16), "seq", scatter_dimension=0, tiled=True
    ).astype(jnp.float32)
    grad_feat_b = grad_feat.astype(jnp.bfloat16)
    input_term = jnp.einsum("tc,cd->td", query_grad, w_query, preferred_element_type=jnp.float32)
    input_term = input_term + jnp.einsum(
        "tc,cd->td", key_grad, w_key, preferred_element_type=jnp.float32
    )
    input_term = input_term + jnp.einsum(
        "tc,cd->td", value_grad, w_value, preferred_element_type=jnp.float32
    )
    input_term = input_term + jnp.einsum(
        "tp,dp->td", grad_feat_b, w_junction, preferred_element_type=jnp.float32
    )
    grad_input = lax.psum_scatter(
        input_term.astype(jnp.bfloat16), "head", scatter_dimension=1, tiled=True
    )
    key_wterm = jnp.einsum("tc,td->cd", key_grad, hidden, preferred_element_type=jnp.float32)
    value_wterm = jnp.einsum("tc,td->cd", value_grad, hidden, preferred_element_type=jnp.float32)
    query_wterm = jnp.einsum("tc,td->cd", query_grad, hidden, preferred_element_type=jnp.float32)
    query_wsum, key_wsum, value_wsum = lax.psum(
        (query_wterm, key_wterm, value_wterm), ("interval", "seq")
    )
    return (
        grad_input[None],
        query_wsum.astype(jnp.bfloat16),
        key_wsum.astype(jnp.bfloat16),
        value_wsum.astype(jnp.bfloat16),
    )


def solution(mesh):
    placed = (
        P("interval", "seq", None),
        P("interval", "seq", "head"),
        P("head", None),
        P("head", None),
        P("head", None),
        P(),
        P("interval", "seq", None, "head"),
        P("interval", "seq", None, "head"),
        P("interval", "seq", None),
        P("interval", "seq", None, "head"),
    )
    return jax.shard_map(
        on_device,
        mesh=mesh,
        in_specs=placed,
        out_specs=(P("interval", "seq", "head"), P("head", None), P("head", None), P("head", None)),
        check_vma=False,
    )
```

profile of v0, /device:TPU:64, one launch (start us, length us, event | category | flops | bytes accessed | tf_op | source)
XLA Modules:
  0.0 447.5 jit_solution(17675293737374444175)
XLA Ops:
  7.2 0.8 squeeze.15
  8.1 0.8 compare_select_fusion
  9.0 0.7 compare_select_fusion.1
  9.8 1.3 convolution_convert_fusion.4
  11.1 13.6 %all_gather.11 = bf16[2048,128]{1,0:T(8,128)(2,1)S(1)} all-gather(bf16[256,128]{1,0:T(8,128)(2,1)S(1)} %convolution_convert_fusion.4), channel_id=1, replica_groups=mesh['interval'=8,'seq'=8,'head'=8] {'seq'}, dimensions={0}, use_global_device_ids=true | all-gather | bytes 589824 | tf_op jit(solution)/shard_map/all_gather | solution.py:42
  24.7 0.6 gather_fusion
  25.4 0.8 squeeze.16
  26.3 0.7 lt.67
  27.1 0.6 gather_fusion.1
  27.9 1.1 scatter_custom_fusion
  29.1 0.8 convert_element_type.105
  30.4 13.4 %all_gather.9 = bf16[2048,192]{0,1:T(8,128)(2,1)S(1)} all-gather(bf16[256,192]{0,1:T(8,128)(2,1)S(1)} %convolution_convert_fusion.3), channel_id=1, replica_groups=mesh['interval'=8,'seq'=8,'head'=8] {'seq'}, dimensions={0}, use_global_device_ids=true | all-gather | bytes 884736 | tf_op jit(solution)/shard_map/all_gather | solution.py:40
  44.6 14.2 %all_gather.10 = bf16[2048,192]{1,0:T(8,128)(2,1)S(1)} all-gather(bf16[256,192]{1,0:T(8,128)(2,1)S(1)} %convolution_convert_fusion.1), channel_id=1, replica_groups=mesh['interval'=8,'seq'=8,'head'=8] {'seq'}, dimensions={0}, use_global_device_ids=true | all-gather | bytes 884736 | tf_op jit(solution)/shard_map/all_gather | solution.py:41
  58.8 0.5 fusion.31
  59.8 0.7 multiply_reduce_fusion
  60.5 0.6 multiply_convert_fusion
  61.1 1.0 copy-done.1
  62.1 1.3 fusion.2
  63.5 2.4 convolution_convert_fusion
  66.1 2.0 fusion.6
  68.1 0.5 fusion.32
  68.6 1.5 reduce-scatter.9.cloned.1.call-done
  70.1 0.8 convert_element_type.106
  70.9 1.1 scatter_custom_fusion.1
  72.0 37.1 %reduce-scatter.5.cloned.1.call-done = bf16[256,192]{0,1:T(8,128)(2,1)} async-done(((bf16[2048,192]{0,1:T(8,128)(2,1)}), bf16[256,192]{0,1:T(8,128)(2,1)}) %reduce-scatter.5.cloned.1.call-update) | async-done | bytes 98320 | tf_op jit(solution)/shard_map/reduce_scatter | solution.py:76
  109.1 2.7 convolution_add_fusion.2
  111.8 35.7 %reduce-scatter.7.cloned.1.call-done = bf16[256,192]{0,1:T(8,128)(2,1)} async-done(((bf16[2048,192]{0,1:T(8,128)(2,1)}), bf16[256,192]{0,1:T(8,128)(2,1)}) %reduce-scatter.7.cloned.1.call-update) | async-done | bytes 98320 | tf_op jit(solution)/shard_map/reduce_scatter | solution.py:79
  147.5 1.9 convolution_add_fusion.1
  149.5 1.3 fusion
  151.1 0.5 copy-done.8
  152.0 1.3 fusion.8
  153.3 287.6 %all-reduce.2 = (bf16[192,1536]{1,0:T(8,128)(2,1)}, bf16[192,1536]{1,0:T(8,128)(2,1)}, bf16[192,1536]{1,0:T(8,128)(2,1)}) all-reduce(f32[192,1536]{1,0:T(8,128)S(1)} %fusion.12, f32[192,1536]{1,0:T(8,128)S(1)} %fusion.10, f32[192,1536]{1,0:T(8,128)} %fusion.8), channel_id=1, replica_groups=mesh['interval'=8,'seq'=8,'head'=8] {'interval','seq'}, use_global_device_ids=true, to_apply=%region_10.11 | all-reduce | flops 884736 | bytes 5308416 | tf_op jit(solution)/shard_map/psum | solution.py:131
  (53 shorter events, 3.3 us)
Async XLA Ops:
  7.2 2.6 copy-start
  7.2 62.9 %reduce-scatter.9.cloned.1.call-start = ((), (), s32[]{:S(2)}) async-start(), calls=%async_computation.6 | async-start | bytes 589824 | tf_op jit(solution)/shard_map/reduce_scatter | solution.py:111
  11.1 18.9 %copy-start.4 = (bf16[192,1536]{1,0:T(8,128)(2,1)S(1)}, bf16[192,1536]{1,0:T(8,128)(2,1)}, u32[]{:S(2)}) copy-start(bf16[192,1536]{1,0:T(8,128)(2,1)} %param.13) | copy-start | bytes 1769476
  29.1 14.7 %copy-start.3 = (bf16[192,1536]{1,0:T(8,128)(2,1)S(1)}, bf16[192,1536]{1,0:T(8,128)(2,1)}, u32[]{:S(2)}) copy-start(bf16[192,1536]{1,0:T(8,128)(2,1)} %param.12) | copy-start | bytes 1769476
  29.9 14.3 %copy-start.6 = (bf16[192,1536]{1,0:T(8,128)(2,1)S(1)}, bf16[192,1536]{1,0:T(8,128)(2,1)}, u32[]{:S(2)}) copy-start(bf16[192,1536]{1,0:T(8,128)(2,1)} %param.14) | copy-start | bytes 1769476
  29.9 79.1 %reduce-scatter.5.cloned.1.call-start = ((), (), s32[]{:S(2)}) async-start(), calls=%async_computation.4 | async-start | bytes 884736 | tf_op jit(solution)/shard_map/reduce_scatter | solution.py:76
  43.8 15.0 %copy-start.2 = (bf16[2048,192]{0,1:T(8,128)(2,1)}, bf16[2048,192]{0,1:T(8,128)(2,1)S(1)}, u32[]{:S(2)}) copy-start(bf16[2048,192]{0,1:T(8,128)(2,1)S(1)} %all_gather.9) | copy-start | bytes 2359300
  58.8 1.0 copy-start.11
  61.1 1.0 copy-start.1
  63.5 2.6 copy-start.10
  63.5 84.0 %reduce-scatter.7.cloned.1.call-start = ((), (), s32[]{:S(2)}) async-start(), calls=%async_computation.5 | async-start | bytes 884736 | tf_op jit(solution)/shard_map/reduce_scatter | solution.py:79
  66.0 375.0 %reduce-scatter.11.cloned.1.call-start = ((), (), s32[]{:S(2)}) async-start(), calls=%async_computation.7 | async-start | bytes 884736 | tf_op jit(solution)/shard_map/reduce_scatter | solution.py:125
  68.6 79.0 %copy-start.7 = (bf16[192,1536]{1,0:T(8,128)(2,1)S(1)}, bf16[192,1536]{1,0:T(8,128)(2,1)}, u32[]{:S(2)}) copy-start(bf16[192,1536]{1,0:T(8,128)(2,1)} %param.14) | copy-start | bytes 1769476
  111.8 37.6 %copy-start.5 = (bf16[1536,128]{1,0:T(8,128)(2,1)S(1)}, bf16[1536,128]{1,0:T(8,128)(2,1)}, u32[]{:S(2)}) copy-start(bf16[1536,128]{1,0:T(8,128)(2,1)} %param.15) | copy-start | bytes 1179652
  150.7 0.9 copy-start.8
  150.8 1.2 copy-start.9
Sparse Core Ops, SparseCore 0:
  30.1 39.9 reduce-scatter.8
  73.1 35.9 reduce-scatter.4
  111.9 35.5 reduce-scatter.6
  151.0 39.1 reduce-scatter.10
where the time goes:
time: 448 us; the launch traced here: 447 us
  blocking collectives  329 us (73%)
  waiting for transfers between devices  74.4 us (17%)
  matrix products  17.9 us (4%)
  between operations  14 us (3%)
  other arithmetic  6.55 us (1%)
  local copies, waits for them, and re-layouts  5.71 us (1%)
    psum x1, blocking collectives, on_device(): lax.psum((query_wterm, key_wterm, value_wterm), ('interval', 'seq'))  288 us
    reduce_scatter x1, waiting for transfers between devices, on_device(): lax.psum_scatter(key_term.astype(jnp.bfloat16), 'seq', scatter_dimension=...  37.1 us
    reduce_scatter x1, waiting for transfers between devices, on_device(): lax.psum_scatter(value_term.astype(jnp.bfloat16), 'seq', scatter_dimensio...  35.7 us
    all_gather x1, blocking collectives, on_device(): lax.all_gather(value_rows, 'seq', axis=0, tiled=True)  14.2 us
    all_gather x1, blocking collectives, on_device(): lax.all_gather(features, 'seq', axis=0, tiled=True)  13.6 us
    all_gather x1, blocking collectives, on_device(): lax.all_gather(key_rows, 'seq', axis=0, tiled=True)  13.4 us
  transfers between devices with their start and end apart: 4, of which 3 were waited for; matrix products, arithmetic and copies ran while one was open for 4% of the time, Pallas kernels for 0%

commit v1 on v0

--- a/solution.py
+++ b/solution.py
@@ -129,7 +129,7 @@
     value_wterm = jnp.einsum("tc,td->cd", value_grad, hidden, preferred_element_type=jnp.float32)
     query_wterm = jnp.einsum("tc,td->cd", query_grad, hidden, preferred_element_type=jnp.float32)
     query_wsum, key_wsum, value_wsum = lax.psum(
-        (query_wterm, key_wterm, value_wterm), ("interval", "seq")
+        lax.psum((query_wterm, key_wterm, value_wterm), "interval"), "seq"
     )
     return (
         grad_input[None],

time: 448 us -> 331 us (0.74)
  the two profiles are of different devices: /device:TPU:64 before, /device:TPU:24 now
where the time goes in v1:
time: 331 us
  waiting for transfers between devices  182 us (55%)
  blocking collectives  100 us (30%)
  matrix products  20.5 us (6%)
  between operations  14.1 us (4%)
  other arithmetic  7.82 us (2%)
  local copies, waits for them, and re-layouts  5.88 us (2%)
    psum x1, waiting for transfers between devices, on_device(): lax.psum((query_wterm, key_wterm, value_wterm), 'interval')  98.1 us
    psum x1, blocking collectives, on_device(): lax.psum(lax.psum((query_wterm, key_wterm, value_wterm), 'interval'), 'seq')  58.6 us
    reduce_scatter x1, waiting for transfers between devices, on_device(): lax.psum_scatter(value_term.astype(jnp.bfloat16), 'seq', scatter_dimensio...  36.5 us
    reduce_scatter x1, waiting for transfers between devices, on_device(): lax.psum_scatter(spread_term.astype(jnp.bfloat16), 'seq', scatter_dimensi...  34.3 us
    all_gather x1, blocking collectives, on_device(): lax.all_gather(features, 'seq', axis=0, tiled=True)  14.2 us
    all_gather x1, blocking collectives, on_device(): lax.all_gather(key_rows, 'seq', axis=0, tiled=True)  13.7 us
    all_gather x1, blocking collectives, on_device(): lax.all_gather(value_rows, 'seq', axis=0, tiled=True)  13.7 us
    reduce_scatter x1, waiting for transfers between devices, on_device(): lax.psum_scatter(key_term.astype(jnp.bfloat16), 'seq', scatter_dimension=...  12.8 us
  transfers between devices with their start and end apart: 5, of which 4 were waited for; matrix products, arithmetic and copies ran while one was open for 8% of the time, Pallas kernels for 0%

profile of v1, /device:TPU:24, one launch (start us, length us, event | category | flops | bytes accessed | tf_op | source)
XLA Modules:
  0.0 330.5 jit_solution(18122075059134062253)
XLA Ops:
  7.2 1.1 copy-done
  8.3 1.5 convolution_convert_fusion.3
  9.8 13.7 %all_gather.9 = bf16[2048,192]{0,1:T(8,128)(2,1)S(1)} all-gather(bf16[256,192]{0,1:T(8,128)(2,1)S(1)} %convolution_convert_fusion.3), channel_id=1, replica_groups=mesh['interval'=8,'seq'=8,'head'=8] {'seq'}, dimensions={0}, use_global_device_ids=true | all-gather | bytes 884736 | tf_op jit(solution)/shard_map/all_gather | solution.py:40
  24.3 13.7 %all_gather.10 = bf16[2048,192]{1,0:T(8,128)(2,1)S(1)} all-gather(bf16[256,192]{1,0:T(8,128)(2,1)S(1)} %convolution_convert_fusion.1), channel_id=1, replica_groups=mesh['interval'=8,'seq'=8,'head'=8] {'seq'}, dimensions={0}, use_global_device_ids=true | all-gather | bytes 884736 | tf_op jit(solution)/shard_map/all_gather | solution.py:41
  38.1 0.5 fusion.31
  39.1 0.7 multiply_reduce_fusion
  39.8 0.6 multiply_convert_fusion
  40.4 1.0 copy-done.1
  41.4 1.3 fusion.2
  42.8 2.4 convolution_convert_fusion
  46.2 1.4 convolution_convert_fusion.4
  47.5 0.6 gather_fusion
  48.2 14.2 %all_gather.11 = bf16[2048,128]{1,0:T(8,128)(2,1)} all-gather(bf16[256,128]{1,0:T(8,128)(2,1)S(1)} %convolution_convert_fusion.4), channel_id=1, replica_groups=mesh['interval'=8,'seq'=8,'head'=8] {'seq'}, dimensions={0}, use_global_device_ids=true | all-gather | bytes 589824 | tf_op jit(solution)/shard_map/all_gather | solution.py:42
  62.4 1.7 gather_fusion.1
  64.2 1.9 scatter_custom_fusion
  66.2 2.1 convert_element_type.105
  68.9 0.6 copy-done.8
  69.5 1.3 fusion.12
  70.8 12.8 %reduce-scatter.5.cloned.1.call-done = bf16[256,192]{0,1:T(8,128)(2,1)} async-done(((bf16[2048,192]{0,1:T(8,128)(2,1)}), bf16[256,192]{0,1:T(8,128)(2,1)}) %reduce-scatter.5.cloned.1.call-update) | async-done | bytes 98320 | tf_op jit(solution)/shard_map/reduce_scatter | solution.py:76
  83.6 2.3 fusion.10
  85.9 36.5 %reduce-scatter.7.cloned.1.call-done = bf16[256,192]{0,1:T(8,128)(2,1)} async-done(((bf16[2048,192]{0,1:T(8,128)(2,1)}), bf16[256,192]{0,1:T(8,128)(2,1)}) %reduce-scatter.7.cloned.1.call-update) | async-done | bytes 98320 | tf_op jit(solution)/shard_map/reduce_scatter | solution.py:79
  122.4 2.2 fusion.8
  124.8 0.5 fusion.28
  125.3 1.3 fusion.32
  126.6 34.3 %reduce-scatter.9.cloned.1.call-done = bf16[256,128]{1,0:T(8,128)(2,1)} async-done(((bf16[2048,128]{1,0:T(8,128)(2,1)}), bf16[256,128]{1,0:T(8,128)(2,1)}) %reduce-scatter.9.cloned.1.call-update) | async-done | bytes 65552 | tf_op jit(solution)/shard_map/reduce_scatter | solution.py:111
  161.0 0.8 convert_element_type.106
  161.8 1.2 scatter_custom_fusion.1
  163.0 1.3 convolution_add_fusion.2
  164.4 1.6 convolution_add_fusion.1
  166.0 1.2 fusion
  167.3 98.1 %all-reduce.5.cloned.1.call-done = (f32[192,1536]{1,0:T(8,128)}, f32[192,1536]{1,0:T(8,128)}, f32[192,1536]{1,0:T(8,128)}) async-done(((f32[192,1536]{1,0:T(8,128)}, f32[192,1536]{1,0:T(8,128)}, f32[192,1536]{1,0:T(8,128)}), (f32[192,1536]{1,0:T(8,128)}, f32[192,1536]{1,0:T(8,128)}, f32[192,1536]{1,0:T(8,128)})) %all-reduce.5.cloned.1.call-update) | async-done | bytes 3538960 | tf_op jit(solution)/shard_map/psum | solution.py:132
  265.4 58.6 %all-reduce.6 = (bf16[192,1536]{1,0:T(8,128)(2,1)}, bf16[192,1536]{1,0:T(8,128)(2,1)}, bf16[192,1536]{1,0:T(8,128)(2,1)}) all-reduce(f32[192,1536]{1,0:T(8,128)} %get-tuple-element.7, f32[192,1536]{1,0:T(8,128)} %get-tuple-element.8, f32[192,1536]{1,0:T(8,128)} %get-tuple-element.9), channel_id=1, replica_groups=mesh['interval'=8,'seq'=8,'head'=8] {'seq'}, use_global_device_ids=true, to_apply=%region_11.12 | all-reduce | flops 884736 | bytes 5308416 | tf_op jit(solution)/shard_map/psum | solution.py:131
  (64 shorter events, 3.1 us)
Async XLA Ops:
  7.2 1.1 copy-start
  7.2 16.3 %copy-start.5 = (bf16[192,1536]{1,0:T(8,128)(2,1)S(1)}, bf16[192,1536]{1,0:T(8,128)(2,1)}, u32[]{:S(2)}) copy-start(bf16[192,1536]{1,0:T(8,128)(2,1)} %param.12) | copy-start | bytes 1769476
  7.2 16.7 %copy-start.9 = (bf16[192,1536]{1,0:T(8,128)(2,1)S(1)}, bf16[192,1536]{1,0:T(8,128)(2,1)}, u32[]{:S(2)}) copy-start(bf16[192,1536]{1,0:T(8,128)(2,1)} %param.14) | copy-start | bytes 1769476
  7.2 76.4 %reduce-scatter.5.cloned.1.call-start = ((), (), s32[]{:S(2)}) async-start(), calls=%async_computation.4 | async-start | bytes 884736 | tf_op jit(solution)/shard_map/reduce_scatter | solution.py:76
  23.5 14.5 %copy-start.3 = (bf16[2048,192]{0,1:T(8,128)(2,1)}, bf16[2048,192]{0,1:T(8,128)(2,1)S(1)}, u32[]{:S(2)}) copy-start(bf16[2048,192]{0,1:T(8,128)(2,1)S(1)} %all_gather.9) | copy-start | bytes 2359300
  38.1 1.0 copy-start.15
  40.4 1.0 copy-start.1
  42.7 2.8 copy-start.10
  42.7 2.8 copy-start.11
  42.7 2.9 copy-start.13
  42.7 3.3 copy-start.14
  42.7 79.6 %reduce-scatter.7.cloned.1.call-start = ((), (), s32[]{:S(2)}) async-start(), calls=%async_computation.5 | async-start | bytes 884736 | tf_op jit(solution)/shard_map/reduce_scatter | solution.py:79
  45.3 115.7 %reduce-scatter.9.cloned.1.call-start = ((), (), s32[]{:S(2)}) async-start(), calls=%async_computation.6 | async-start | bytes 589824 | tf_op jit(solution)/shard_map/reduce_scatter | solution.py:111
  47.5 20.8 %copy-start.2 = (bf16[256,2048]{1,0:T(8,128)(2,1)S(1)}, bf16[256,2048]{1,0:T(8,128)(2,1)}, u32[]{:S(2)}) copy-start(bf16[256,2048]{1,0:T(8,128)(2,1)} %copy-done.1) | copy-start | bytes 3145732
  47.5 20.8 %copy-start.4 = (bf16[2048,192]{0,1:T(8,128)(2,1)S(1)}, bf16[2048,192]{0,1:T(8,128)(2,1)}, u32[]{:S(2)}) copy-start(bf16[2048,192]{0,1:T(8,128)(2,1)} %copy-done.3) | copy-start | bytes 2359300
  64.2 4.6 %copy-start.12 = (f32[64]{0:T(128)}, f32[64]{0:T(128)S(1)}, u32[]{:S(2)}) copy-start(f32[64]{0:T(128)S(1)} %fusion.29) | copy-start | bytes 772
  68.3 197.2 %all-reduce.5.cloned.1.call-start = ((), (), s32[]{:S(2)}) async-start(), calls=%async_computation.8 | async-start | bytes 7077888 | tf_op jit(solution)/shard_map/psum | solution.py:132
  68.8 0.6 copy-start.8
  124.6 38.4 %copy-start.6 = (bf16[192,1536]{1,0:T(8,128)(2,1)S(1)}, bf16[192,1536]{1,0:T(8,128)(2,1)}, u32[]{:S(2)}) copy-start(bf16[192,1536]{1,0:T(8,128)(2,1)} %param.13) | copy-start | bytes 1769476
  124.6 199.3 %reduce-scatter.11.cloned.1.call-start = ((), (), s32[]{:S(2)}) async-start(), calls=%async_computation.7 | async-start | bytes 884736 | tf_op jit(solution)/shard_map/reduce_scatter | solution.py:125
  164.4 1.6 copy-start.7
Sparse Core Ops, SparseCore 0:
  42.8 40.7 reduce-scatter.4
  86.7 35.6 reduce-scatter.6
  125.7 35.1 reduce-scatter.8
  163.6 101.8 all-reduce.4
  268.7 40.4 reduce-scatter.10
